TPU v7x, 256 devices: a whole 4x4x8 slice. The times are simulated.
256 devices in a mesh: af: 64 (over y_hi, z, x), row: 4 (over y_lo, core).
Axes of the slice: x: 4, y: 4 (y_hi: 2, y_lo: 2; y = y_hi * 2 + y_lo), z: 8, core: 2. Of those that a mesh axis runs over, the one named last changes fastest.
Arguments:
- source_traces: bfloat16 [512, 1024, 2048], P('af', 'row'), may hold values from -6 to 6
- receiver_traces: bfloat16 [128, 1024, 2048], P('row', 'af'), may hold values from -6 to 6
- wavelet_inverse: float32 [64, 2], replicated, may hold values from -4 to 4
Outputs:
- multiples: bfloat16 [512, 128, 2048], P('af', 'row')
All inputs are finite; a program needn't handle non-finite values.
Results may differ from a plain program's by a relative error of at most 0.008.
Values may be sent and summed in bfloat16 or wider, within the bound.
No kernel may reach another device: no remote copies, remote signals or barrier semaphores. Data moves between devices by JAX's collectives and lax.ppermute only.
A program may use at most 64 MiB of HBM per device.

v0:
```python
import math
import jax
import jax.numpy as jnp
from jax import lax
from jax.sharding import PartitionSpec as P

NT = 2048
NF = 64
F_LOW = 96
K = 1024


def tables(amplitude):
    samples = jnp.arange(NT, dtype=jnp.int32)
    frequency = F_LOW + jnp.arange(NF, dtype=jnp.int32)
    phase_index = frequency[:, None] * samples[None, :] % NT
    angles = phase_index.astype(jnp.float32) * (2.0 * math.pi / NT)
    return jnp.stack([jnp.cos(angles) * amplitude, -jnp.sin(angles) * amplitude], axis=1).astype(
        jnp.bfloat16
    )


def coupling(recv_block):
    rcv_real = recv_block[:, 0]
    rcv_imag = recv_block[:, 1]
    real_row = jnp.stack([rcv_real, -rcv_imag], axis=1)
    imag_row = jnp.stack([rcv_imag, rcv_real], axis=1)
    return jnp.stack([real_row, imag_row], axis=1)


def per_device(source_traces, receiver_traces, wavelet_inverse):
    forward = tables(1.0 / math.sqrt(NT))
    source_spec = jnp.einsum(
        "fct,skt->fcsk", forward, source_traces, preferred_element_type=jnp.float32
    ).astype(jnp.bfloat16)
    receiver_spec = jnp.einsum(
        "fct,rkt->fckr", forward, receiver_traces, preferred_element_type=jnp.float32
    ).astype(jnp.bfloat16)
    source_freq, receiver_freq = (
        lax.all_to_all(source_spec, "af", split_axis=0, concat_axis=2, tiled=True),
        lax.all_to_all(receiver_spec, "af", split_axis=0, concat_axis=2, tiled=True),
    )
    local_freqs = source_freq.shape[0]
    raw = jnp.einsum(
        "fockr,fcsk->rfos",
        coupling(receiver_freq),
        lax.all_gather(source_freq, "row", axis=3, tiled=True),
        preferred_element_type=jnp.float32,
    )
    first_freq = lax.axis_index("af") * local_freqs
    wavelet_rows = lax.dynamic_slice_in_dim(wavelet_inverse, first_freq, local_freqs, 0)
    wave_real = wavelet_rows[:, 0][None, :, None]
    wave_imag = wavelet_rows[:, 1][None, :, None]
    raw_real = raw[:, :, 0, :]
    raw_imag = raw[:, :, 1, :]
    amplitude = 1.0 / math.sqrt(K)
    pred_real = (raw_real * wave_real - raw_imag * wave_imag) * amplitude
    pred_imag = (raw_real * wave_imag + raw_imag * wave_real) * amplitude
    predicted = jnp.stack([pred_real, pred_imag], axis=2).astype(jnp.bfloat16)
    returned = lax.all_to_all(predicted, "af", split_axis=3, concat_axis=1, tiled=True)
    inverse = tables(1.0 / math.sqrt(NF))
    result = jnp.einsum("rfcs,fct->srt", returned, inverse, preferred_element_type=jnp.float32)
    return result.astype(jnp.bfloat16)


def solution(mesh):
    return jax.shard_map(
        per_device,
        mesh=mesh,
        in_specs=(P("af", "row", None), P("row", "af", None), P()),
        out_specs=P("af", "row", None),
        check_vma=False,
    )
```

profile of v0, /device:TPU:1, one launch (start us, length us, event | category | flops | bytes accessed | tf_op | source)
XLA Modules:
  0.0 115.3 jit_solution(388761204805325706)
XLA Ops:
  6.5 2.5 %multiply_convert_fusion.1 = (bf16[64,1,2048]{2,0,1:T(8,128)(2,1)S(1)}, bf16[64,1,2048]{2,0,1:T(8,128)(2,1)S(1)}, bf16[64,1,2048]{2,0,1:T(8,128)(2,1)S(1)}, bf16[64,1,2048]{2,0,1:T(8,128)(2,1)S(1)}) fusion(s32[64]{0:T(128)S(1)} %iota_add_fusion), kind=kLoop, calls=%fused_computation.26 | loop fusion | flops 3014656 | bytes 1048832 | tf_op jit(solution)/shard_map/convert.2
  9.1 6.3 %fusion.9 = bf16[64,2,8,256]{3,0,2,1:T(8,128)(2,1)S(1)} fusion(bf16[8,256,2048]{2,1,0:T(8,128)(2,1)} %param.3, bf16[64,1,2048]{2,0,1:T(8,128)(2,1)S(1)} %get-tuple-element.15, bf16[64,1,2048]{2,0,1:T(8,128)(2,1)S(1)} %get-tuple-element.13), kind=kOutput, calls=%fused_computation.10 | convolution fusion | flops 1075052544 | bytes 9437184 | tf_op jit(solution)/shard_map/fct,skt->fcsk/dot_general | solution.py:33
  15.3 0.3 copy.13
  15.6 32.5 %all_to_all.54 = bf16[64,2,8,256]{3,2,1,0:T(8,128)(2,1)S(1)} all-to-all(bf16[64,2,8,256]{3,2,1,0:T(8,128)(2,1)S(1)} %copy.13), channel_id=1, replica_groups=mesh['af'=64,'row'=4] {'af'}, dimensions={0} | all-to-all | bytes 1048576 | tf_op jit(solution)/shard_map/all_to_all | solution.py:40
  48.1 0.8 copy.39
  49.0 1.5 %fusion.15 = bf16[64,2,16,32]{0,3,2,1:T(8,128)(2,1)S(1)} fusion(bf16[32,16,2048]{2,1,0:T(8,128)(2,1)S(1)} %copy-done.1, bf16[64,1,2048]{2,0,1:T(8,128)(2,1)S(1)} %get-tuple-element.15, bf16[64,1,2048]{2,0,1:T(8,128)(2,1)S(1)} %get-tuple-element.13), kind=kOutput, calls=%fused_computation.12 | convolution fusion | flops 269549568 | bytes 2752512 | tf_op jit(solution)/shard_map/fct,rkt->fckr/dot_general | solution.py:36
  50.5 0.8 copy.16
  51.3 1.1 reshape.223
  52.4 6.9 %all-to-all-start.1 = ((bf16[64,2,512]{2,1,0:T(2,128)(2,1)}), bf16[64,2,512]{2,1,0:T(2,128)(2,1)S(1)}, u32[]{:S(2)}, u32[]{:S(2)}) async-start(bf16[64,2,512]{2,1,0:T(2,128)(2,1)} %reshape.223), calls=%async_computation.1 | async-start | bytes 262144 | tf_op jit(solution)/shard_map/all_to_all | solution.py:41
  59.3 0.1 constant_dynamic-slice_fusion
  59.4 0.6 fusion.38
  60.0 10.8 %all-to-all-done.1 = bf16[64,2,512]{2,1,0:T(2,128)(2,1)S(1)} async-done(((bf16[64,2,512]{2,1,0:T(2,128)(2,1)}), bf16[64,2,512]{2,1,0:T(2,128)(2,1)S(1)}, u32[]{:S(2)}, u32[]{:S(2)}) %all-to-all-start.1) | async-done | bytes 131104 | tf_op jit(solution)/shard_map/all_to_all | solution.py:41
  70.8 0.3 reshape.224
  71.2 0.1 copy.29
  71.3 0.1 copy.28
  71.5 7.5 %all-gather.2.cloned.1.call-done = bf16[1,2,512,1024]{3,2,1,0:T(8,128)(2,1)} async-done(((bf16[1,2,512,256]{3,2,1,0:T(8,128)(2,1)}), bf16[1,2,512,1024]{3,2,1,0:T(8,128)(2,1)}) %all-gather.2.cloned.1.call-update) | async-done | bytes 2097168 | tf_op jit(solution)/shard_map/all_gather | solution.py:47
  79.0 2.4 %fusion.18 = f32[32,1,2,512]{3,0,2,1:T(8,128)S(1)} fusion(bf16[1,2,512,1024]{3,2,1,0:T(8,128)(2,1)} %all-gather.2.cloned.1.call-done, bf16[1,1,2,1024,32]{3,4,2,1,0:T(8,128)(2,1)S(1)} %get-tuple-element.10, bf16[1,1,2,1024,32]{3,4,2,1,0:T(8,128)(2,1)S(1)} %get-tuple-element.9), kind=kOutput, calls=%fused_computation.13 | convolution fusion | flops 134742016 | bytes 2490368 | tf_op jit(solution)/shard_map/fockr,fcsk->rfos/dot_general | solution.py:44
  81.4 1.3 %multiply_convert_fusion.5 = (bf16[32,1,1,512]{3,0,2,1:T(8,128)(2,1)S(1)}, bf16[32,1,1,512]{3,0,2,1:T(8,128)(2,1)S(1)}) fusion(f32[32,1,2,512]{3,0,2,1:T(8,128)S(1)} %fusion.18, f32[]{:T(128)} %bitcast.24, f32[]{:T(128)} %bitcast.22), kind=kLoop, calls=%fused_computation.42 | loop fusion | flops 163840 | bytes 196616 | tf_op jit(solution)/shard_map/convert
  82.6 0.2 copy.20
  82.8 0.2 reshape.225
  83.0 23.5 %all_to_all.55 = bf16[64,2,256]{2,1,0:T(2,128)(2,1)S(1)} all-to-all(bf16[64,2,256]{2,1,0:T(2,128)(2,1)S(1)} %reshape.225), channel_id=1, replica_groups=mesh['af'=64,'row'=4] {'af'}, dimensions={0} | all-to-all | bytes 131072 | tf_op jit(solution)/shard_map/all_to_all | solution.py:60
  106.5 0.2 reshape.226
  106.7 0.3 copy.22
  107.0 1.4 %fusion.3 = bf16[8,32,2048]{2,1,0:T(8,128)(2,1)} fusion(bf16[64,1,2048]{2,0,1:T(8,128)(2,1)S(1)} %get-tuple-element.14, bf16[64,1,2048]{2,0,1:T(8,128)(2,1)S(1)} %get-tuple-element.16, bf16[32,1,2,64,8]{3,0,2,4,1:T(8,128)(2,1)S(1)} %copy.22), kind=kOutput, calls=%fused_computation.4 | convolution fusion | flops 135790592 | bytes 1638400 | tf_op jit(solution)/shard_map/rfcs,fct->srt/dot_general | solution.py:62
  (12 shorter events, 0.2 us)
Async XLA Ops:
  6.5 52.8 %copy-start = (f32[64,2]{0,1:T(2,128)S(1)}, f32[64,2]{0,1:T(2,128)}, u32[]{:S(2)}) copy-start(f32[64,2]{0,1:T(2,128)} %param.5) | copy-start | bytes 1540
  6.5 72.5 %all-gather.2.cloned.1.call-start = ((), (), s32[]{:S(2)}) async-start(), calls=%async_computation.3 | async-start | bytes 2621440 | tf_op jit(solution)/shard_map/all_gather | solution.py:47
  15.3 33.7 %copy-start.1 = (bf16[32,16,2048]{2,1,0:T(8,128)(2,1)S(1)}, bf16[32,16,2048]{2,1,0:T(8,128)(2,1)}, u32[]{:S(2)}) copy-start(bf16[32,16,2048]{2,1,0:T(8,128)(2,1)} %param.4) | copy-start | bytes 6291460
  52.4 18.4 %all-to-all-start.1 = ((bf16[64,2,512]{2,1,0:T(2,128)(2,1)}), bf16[64,2,512]{2,1,0:T(2,128)(2,1)S(1)}, u32[]{:S(2)}, u32[]{:S(2)}) async-start(bf16[64,2,512]{2,1,0:T(2,128)(2,1)} %reshape.223), calls=%async_computation.1 | async-start | bytes 262144 | tf_op jit(solution)/shard_map/all_to_all | solution.py:41
Sparse Core Ops, SparseCore 0:
  49.1 29.8 all-gather.1
where the time goes:
time: 116 us; the launch traced here: 115 us
  blocking collectives  56 us (48%)
  waiting for transfers between devices  18.3 us (16%)
  between operations  13.5 us (12%)
  matrix products  11.6 us (10%)
  starting transfers between devices  6.93 us (6%)
  local copies, waits for them, and re-layouts  5.02 us (4%)
  other arithmetic  3.83 us (3%)
    all_to_all x1, blocking collectives, per_device(): lax.all_to_all(source_spec, 'af', split_axis=0, concat_axis=2, tiled=True)  32.5 us
    all_to_all x1, blocking collectives, per_device(): lax.all_to_all(predicted, 'af', split_axis=3, concat_axis=1, tiled=True)  23.5 us
    all_to_all x1, waiting for transfers between devices, per_device(): lax.all_to_all(receiver_spec, 'af', split_axis=0, concat_axis=2, tiled=True)  10.8 us
    all_gather x1, waiting for transfers between devices, per_device(): lax.all_gather(source_freq, 'row', axis=3, tiled=True)  7.53 us
    all_to_all x1, starting transfers between devices, per_device(): lax.all_to_all(receiver_spec, 'af', split_axis=0, concat_axis=2, tiled=True)  6.92 us
    dot_general x1, matrix products, per_device(): jnp.einsum('fct,skt->fcsk', forward, source_traces, preferred_element_typ...  6.26 us
    another operation x2, other arithmetic  3.78 us
    dot_general x1, matrix products, per_device(): jnp.einsum('fockr,fcsk->rfos', coupling(receiver_freq), lax.all_gather(so...  2.35 us
  transfers between devices with their start and end apart: 2, of which 2 were waited for; matrix products, arithmetic and copies ran while one was open for 4% of the time, Pallas kernels for 0%

commit v1 on v0

--- a/solution.py
+++ b/solution.py
@@ -44,7 +44,9 @@
     raw = jnp.einsum(
         "fockr,fcsk->rfos",
         coupling(receiver_freq),
-        lax.all_gather(source_freq, "row", axis=3, tiled=True),
+        jnp.concatenate(
+            lax.all_to_all(jnp.stack([source_freq] * lax.axis_size("row")), "row", 0, 0), axis=3
+        ),
         preferred_element_type=jnp.float32,
     )
     first_freq = lax.axis_index("af") * local_freqs

time: 116 us -> 120 us (1.034)
  blocking collectives: 56 us -> 14.9 us
  waiting for transfers between devices: 18.3 us -> 47.4 us
  starting transfers between devices: 6.93 us -> 28.5 us
  between operations: 13.5 us -> 0.15 us
  local copies, waits for them, and re-layouts: 5.02 us -> 12.6 us
    all_to_all x0 -> x2, waiting for transfers between devices: none -> 36 us  [the longest x1 23.5 us: per_device(): lax.all_to_all(jnp.stack([source_freq] * lax.axis_size('row')), 'row', 0, 0)]
    all_to_all x1 -> x0, blocking collectives: 32.5 us -> none  [per_device(): lax.all_to_all(source_spec, 'af', split_axis=0, concat_axis=2, tiled=True)]
    all_to_all x0 -> x2, starting transfers between devices: none -> 21.6 us  [the longest x1 15.1 us: per_device(): lax.all_to_all(source_spec, 'af', split_axis=0, concat_axis=2, tiled=True)]
    all_to_all x1, blocking collectives: 23.5 us -> 14.9 us  [per_device(): lax.all_to_all(predicted, 'af', split_axis=3, concat_axis=1, tiled=True)]
    all_gather x1 -> x0, waiting for transfers between devices: 7.53 us -> none  [per_device(): lax.all_gather(source_freq, 'row', axis=3, tiled=True)]
    another operation x0 -> x2, local copies, waits for them, and re-layouts: none -> 4.7 us
    reshape x0 -> x1, local copies, waits for them, and re-layouts: none -> 2.95 us  [per_device(): jnp.concatenate(lax.all_to_all(jnp.stack([source_freq] * lax.axis_size('r...]
    dot_general x1, matrix products: 2.35 us -> 0.76 us  [per_device(): jnp.einsum('fockr,fcsk->rfos', coupling(receiver_freq), jnp.concatenate(l...]
  transfers between devices with their start and end apart: 2 -> 3, of which waited for: 2 -> 3; matrix products, arithmetic and copies ran while one was open for 4% -> 5% of each run, Pallas kernels for 0% -> 0%
where the time goes in v1:
time: 120 us; the launch traced here: 119 us
  waiting for transfers between devices  47.4 us (40%)
  starting transfers between devices  28.5 us (24%)
  blocking collectives  14.9 us (12%)
  local copies, waits for them, and re-layouts  12.6 us (10%)
  matrix products  11.5 us (10%)
  other arithmetic  3.93 us (3%)
    all_to_all x1, waiting for transfers between devices, per_device(): lax.all_to_all(jnp.stack([source_freq] * lax.axis_size('row')), 'row', 0, 0)  23.5 us
    all_to_all x1, starting transfers between devices, per_device(): lax.all_to_all(source_spec, 'af', split_axis=0, concat_axis=2, tiled=True)  15.1 us
    all_to_all x1, blocking collectives, per_device(): lax.all_to_all(predicted, 'af', split_axis=3, concat_axis=1, tiled=True)  14.9 us
    all_to_all x1, waiting for transfers between devices, per_device(): lax.all_to_all(source_spec, 'af', split_axis=0, concat_axis=2, tiled=True)  12.5 us
    all_to_all x1, waiting for transfers between devices, per_device(): lax.all_to_all(receiver_spec, 'af', split_axis=0, concat_axis=2, tiled=True)  11.4 us
    all_to_all x1, starting transfers between devices, per_device(): lax.all_to_all(receiver_spec, 'af', split_axis=0, concat_axis=2, tiled=True)  6.92 us
    all_to_all x1, starting transfers between devices, per_device(): lax.all_to_all(jnp.stack([source_freq] * lax.axis_size('row')), 'row', 0, 0)  6.48 us
    dot_general x1, matrix products, per_device(): jnp.einsum('fct,skt->fcsk', forward, source_traces, preferred_element_typ...  6.26 us
  transfers between devices with their start and end apart: 3, of which 3 were waited for; matrix products, arithmetic and copies ran while one was open for 5% of the time, Pallas kernels for 0%

profile of v1, /device:TPU:1, one launch (start us, length us, event | category | flops | bytes accessed | tf_op | source)
XLA Modules:
  0.0 119.1 jit_solution(17414040502436916811)
XLA Ops:
  0.0 2.5 %multiply_convert_fusion.1 = (bf16[64,1,2048]{2,0,1:T(8,128)(2,1)S(1)}, bf16[64,1,2048]{2,0,1:T(8,128)(2,1)S(1)}, bf16[64,1,2048]{2,0,1:T(8,128)(2,1)S(1)}, bf16[64,1,2048]{2,0,1:T(8,128)(2,1)S(1)}) fusion(s32[64]{0:T(128)S(1)} %iota_add_fusion), kind=kLoop, calls=%fused_computation.24 | loop fusion | flops 3014656 | bytes 1048832 | tf_op jit(solution)/shard_map/convert.2
  2.5 6.3 %fusion.7 = bf16[64,2,8,256]{3,0,2,1:T(8,128)(2,1)S(1)} fusion(bf16[8,256,2048]{2,1,0:T(8,128)(2,1)} %param.3, bf16[64,1,2048]{2,0,1:T(8,128)(2,1)S(1)} %get-tuple-element.15, bf16[64,1,2048]{2,0,1:T(8,128)(2,1)S(1)} %get-tuple-element.13), kind=kOutput, calls=%fused_computation.8 | convolution fusion | flops 1075052544 | bytes 9437184 | tf_op jit(solution)/shard_map/fct,skt->fcsk/dot_general | solution.py:33
  8.8 1.1 copy.13
  9.9 15.1 %all-to-all-start = ((bf16[64,2,8,256]{3,2,1,0:T(8,128)(2,1)}), bf16[64,2,8,256]{3,2,1,0:T(8,128)(2,1)S(1)}, u32[]{:S(2)}, u32[]{:S(2)}) async-start(bf16[64,2,8,256]{3,2,1,0:T(8,128)(2,1)} %copy.13), calls=%async_computation | async-start | bytes 1048576 | tf_op jit(solution)/shard_map/all_to_all | solution.py:40
  25.0 3.1 %fusion.13 = bf16[64,2,16,32]{0,3,2,1:T(8,128)(2,1)S(1)} fusion(bf16[32,16,2048]{2,1,0:T(8,128)(2,1)} %param.4, bf16[64,1,2048]{2,0,1:T(8,128)(2,1)S(1)} %get-tuple-element.15, bf16[64,1,2048]{2,0,1:T(8,128)(2,1)S(1)} %get-tuple-element.13), kind=kOutput, calls=%fused_computation.10 | convolution fusion | flops 269549568 | bytes 2752512 | tf_op jit(solution)/shard_map/fct,rkt->fckr/dot_general | solution.py:36
  28.1 0.8 copy.17
  28.9 1.1 reshape.235
  29.9 12.5 %all-to-all-done = bf16[64,2,8,256]{3,2,1,0:T(8,128)(2,1)S(1)} async-done(((bf16[64,2,8,256]{3,2,1,0:T(8,128)(2,1)}), bf16[64,2,8,256]{3,2,1,0:T(8,128)(2,1)S(1)}, u32[]{:S(2)}, u32[]{:S(2)}) %all-to-all-start) | async-done | bytes 524320 | tf_op jit(solution)/shard_map/all_to_all | solution.py:40
  42.5 6.9 %all-to-all-start.2 = ((bf16[64,2,512]{2,1,0:T(2,128)(2,1)}), bf16[64,2,512]{2,1,0:T(2,128)(2,1)S(1)}, u32[]{:S(2)}, u32[]{:S(2)}) async-start(bf16[64,2,512]{2,1,0:T(2,128)(2,1)} %reshape.235), calls=%async_computation.2 | async-start | bytes 262144 | tf_op jit(solution)/shard_map/all_to_all | solution.py:41
  49.4 11.4 %all-to-all-done.2 = bf16[64,2,512]{2,1,0:T(2,128)(2,1)S(1)} async-done(((bf16[64,2,512]{2,1,0:T(2,128)(2,1)}), bf16[64,2,512]{2,1,0:T(2,128)(2,1)S(1)}, u32[]{:S(2)}, u32[]{:S(2)}) %all-to-all-start.2) | async-done | bytes 131104 | tf_op jit(solution)/shard_map/all_to_all | solution.py:41
  60.9 1.5 %stack.45 = bf16[4,1,2,512,256]{4,3,2,1,0:T(8,128)(2,1)} broadcast(bf16[2,512,256]{2,1,0:T(8,128)(2,1)S(1)} %bitcast.69), dimensions={2,3,4} | broadcast | bytes 2621440 | tf_op jit(solution)/shard_map/stack | solution.py:48
  62.3 6.5 %all-to-all-start.1 = ((bf16[4,1,2,512,256]{4,3,2,1,0:T(8,128)(2,1)}), bf16[4,1,2,512,256]{4,3,2,1,0:T(8,128)(2,1)S(1)}, u32[]{:S(2)}, u32[]{:S(2)}) async-start(bf16[4,1,2,512,256]{4,3,2,1,0:T(8,128)(2,1)} %stack.45), calls=%async_computation.1 | async-start | bytes 4194304 | tf_op jit(solution)/shard_map/all_to_all | solution.py:48
  68.9 0.6 fusion.33
  69.5 0.3 reshape.236
  70.1 23.5 %all-to-all-done.1 = bf16[4,1,2,512,256]{4,3,2,1,0:T(8,128)(2,1)S(1)} async-done(((bf16[4,1,2,512,256]{4,3,2,1,0:T(8,128)(2,1)}), bf16[4,1,2,512,256]{4,3,2,1,0:T(8,128)(2,1)S(1)}, u32[]{:S(2)}, u32[]{:S(2)}) %all-to-all-start.1) | async-done | bytes 2097184 | tf_op jit(solution)/shard_map/all_to_all | solution.py:48
  93.6 2.9 %copy.15 = bf16[1,2,512,4,256]{4,3,2,1,0:T(4,128)(2,1)} copy(bf16[1,2,512,4,256]{4,2,1,0,3:T(8,128)(2,1)S(1)} %bitcast.68) | data formatting | bytes 4194304 | tf_op jit(solution)/shard_map/reshape | solution.py:47
  96.6 3.2 %reshape.230 = bf16[2,512,1024,1]{2,1,0,3:T(8,128)(2,1)S(1)} reshape(bf16[1,2,512,4,256]{4,3,2,1,0:T(4,128)(2,1)} %copy.15) | data formatting | bytes 4194304 | tf_op jit(solution)/shard_map/reshape.4
  99.8 0.8 convolution_bitcast_fusion.1
  100.6 1.3 %multiply_convert_fusion.5 = (bf16[32,1,1,512]{3,0,2,1:T(8,128)(2,1)S(1)}, bf16[32,1,1,512]{3,0,2,1:T(8,128)(2,1)S(1)}) fusion(f32[32,1,2,512]{3,0,2,1:T(8,128)S(1)} %convolution_bitcast_fusion.1, f32[]{:T(128)} %bitcast.23, f32[]{:T(128)} %bitcast.21), kind=kLoop, calls=%fused_computation.40 | loop fusion | flops 163840 | bytes 196616 | tf_op jit(solution)/shard_map/convert
  102.1 0.2 reshape.237
  102.3 14.9 %all_to_all.56 = bf16[64,2,256]{2,1,0:T(2,128)(2,1)S(1)} all-to-all(bf16[64,2,256]{2,1,0:T(2,128)(2,1)S(1)} %reshape.237), channel_id=1, replica_groups=mesh['af'=64,'row'=4] {'af'}, dimensions={0} | all-to-all | bytes 131072 | tf_op jit(solution)/shard_map/all_to_all | solution.py:62
  117.2 0.2 reshape.238
  117.4 0.3 copy.23
  117.7 1.4 %fusion.3 = bf16[8,32,2048]{2,1,0:T(8,128)(2,1)} fusion(bf16[64,1,2048]{2,0,1:T(8,128)(2,1)S(1)} %get-tuple-element.14, bf16[64,1,2048]{2,0,1:T(8,128)(2,1)S(1)} %get-tuple-element.16, bf16[32,1,2,64,8]{3,0,2,4,1:T(8,128)(2,1)S(1)} %copy.23), kind=kOutput, calls=%fused_computation.4 | convolution fusion | flops 135790592 | bytes 1638400 | tf_op jit(solution)/shard_map/rfcs,fct->srt/dot_general | solution.py:64
  (13 shorter events, 0.6 us)
Async XLA Ops:
  0.0 68.8 %copy-start = (f32[64,2]{0,1:T(2,128)S(1)}, f32[64,2]{0,1:T(2,128)}, u32[]{:S(2)}) copy-start(f32[64,2]{0,1:T(2,128)} %param.5) | copy-start | bytes 1540
  9.9 32.6 %all-to-all-start = ((bf16[64,2,8,256]{3,2,1,0:T(8,128)(2,1)}), bf16[64,2,8,256]{3,2,1,0:T(8,128)(2,1)S(1)}, u32[]{:S(2)}, u32[]{:S(2)}) async-start(bf16[64,2,8,256]{3,2,1,0:T(8,128)(2,1)} %copy.13), calls=%async_computation | async-start | bytes 1048576 | tf_op jit(solution)/shard_map/all_to_all | solution.py:40
  42.5 18.4 %all-to-all-start.2 = ((bf16[64,2,512]{2,1,0:T(2,128)(2,1)}), bf16[64,2,512]{2,1,0:T(2,128)(2,1)S(1)}, u32[]{:S(2)}, u32[]{:S(2)}) async-start(bf16[64,2,512]{2,1,0:T(2,128)(2,1)} %reshape.235), calls=%async_computation.2 | async-start | bytes 262144 | tf_op jit(solution)/shard_map/all_to_all | solution.py:41
  62.3 31.3 %all-to-all-start.1 = ((bf16[4,1,2,512,256]{4,3,2,1,0:T(8,128)(2,1)}), bf16[4,1,2,512,256]{4,3,2,1,0:T(8,128)(2,1)S(1)}, u32[]{:S(2)}, u32[]{:S(2)}) async-start(bf16[4,1,2,512,256]{4,3,2,1,0:T(8,128)(2,1)} %stack.45), calls=%async_computation.1 | async-start | bytes 4194304 | tf_op jit(solution)/shard_map/all_to_all | solution.py:48
